TPU v7x, 256 devices: a whole 4x4x8 slice. The times are simulated.
256 devices in a mesh: ctx: 16 (over y_hi, x, core), head: 16 (over y_lo, z).
Axes of the slice: x: 4, y: 4 (y_hi: 2, y_lo: 2; y = y_hi * 2 + y_lo), z: 8, core: 2. Of those that a mesh axis runs over, the one named last changes fastest.
Arguments:
- queries: bfloat16 [16384, 4096], P('ctx', 'head'), may hold values from -8 to 8
- keys: bfloat16 [16384, 1024], P('ctx'), may hold values from -8 to 8
- values: bfloat16 [16384, 1024], P('ctx'), may hold values from -8 to 8
- grad_out: bfloat16 [16384, 4096], P('ctx', 'head'), may hold values from -8 to 8
- block_index: int32 [16, 4], replicated, may hold values from 0 to 3
Outputs:
- grad_queries: bfloat16 [16384, 4096], P(('ctx', 'head'))
- grad_keys: bfloat16 [16384, 1024], P(('ctx', 'head'))
- grad_values: bfloat16 [16384, 1024], P(('ctx', 'head'))
Inputs may be any that keep to these rules, and one draw needn't show every extreme that they name: block_index[c, l] is read only where c >= 2**l.
All inputs are finite; a program needn't handle non-finite values.
Results may differ from a plain program's by a relative error of at most 0.023.
Values may be sent and summed in bfloat16 or wider, within the bound.
No kernel may reach another device: no remote copies, remote signals or barrier semaphores. Data moves between devices by JAX's collectives and lax.ppermute only.
A program may use at most 64 MiB of HBM per device.

v0:
```python
import jax
import jax.numpy as jnp
from jax import lax
from jax.experimental import pallas as pl
from jax.experimental.pallas import tpu as pltpu
from jax.sharding import PartitionSpec as P


HD = 128
BLK = 256
NEG = -1e30
SCALE = HD**-0.5
FACTOR = SCALE * 1.4426950408889634
HBM = pl.BlockSpec(memory_space=pltpu.HBM)
VMEM = pl.BlockSpec(memory_space=pltpu.VMEM)
SMEM = pl.BlockSpec(memory_space=pltpu.SMEM)


def rotate(value, axis, steps):
    count = lax.axis_size(axis)
    return lax.ppermute(value, axis, [(source, (source + steps) % count) for source in range(count)])


def swap(value, axis):
    return lax.ppermute(value, axis, [(source, source ^ 1) for source in range(lax.axis_size(axis))])


def block_start(index_ref, ctx_index, level_num, ctx_count):
    target = jnp.minimum(ctx_index + 2**level_num, ctx_count - 1)
    return pl.multiple_of(index_ref[level_num, target] * BLK, BLK)


def gather_blocks(block_index, keys, values, ctx_count, levels):
    def body(index_hbm, key_ref, value_ref, own_ref, *refs):
        sends, index_ref, sems = refs[:levels], refs[levels], refs[levels + 1]
        begin = pl.multiple_of(lax.axis_index("head") // 2 * HD, HD)
        started = [pltpu.make_async_copy(index_hbm, index_ref, sems.at[2])]
        for half, source in ((0, key_ref), (1, value_ref)):
            started.append(
                pltpu.make_async_copy(
                    source.at[:, pl.ds(begin, HD)], own_ref.at[:, half * HD : (half + 1) * HD], sems.at[half]
                )
            )
        for copy in started:
            copy.start()
        for copy in started:
            copy.wait()
        ctx_index = lax.axis_index("ctx")
        for level_num in range(levels):
            start = block_start(index_ref, ctx_index, level_num, ctx_count)
            sends[level_num][...] = own_ref[pl.ds(start, BLK), :]

    return pl.pallas_call(
        body,
        out_shape=(jax.ShapeDtypeStruct((keys.shape[0], 2 * HD), keys.dtype),)
        + (jax.ShapeDtypeStruct((BLK, 2 * HD), keys.dtype),) * levels,
        in_specs=[HBM, HBM, HBM],
        out_specs=(VMEM,) * (levels + 1),
        scratch_shapes=[pltpu.SMEM(block_index.shape, jnp.int32), pltpu.SemaphoreType.DMA((3,))],
        compiler_params=params(4),
        name="gather_blocks",
    )(block_index, keys, values)


def dot(left, right):
    return jnp.dot(left, right, preferred_element_type=jnp.float32)


def spot(number):
    return slice(number * BLK, (number + 1) * BLK)


def params(mib):
    return pltpu.CompilerParams(vmem_limit_bytes=mib << 20)


def cost(dots, nbytes):
    return pl.CostEstimate(flops=dots * 2 * BLK * BLK * HD, bytes_accessed=nbytes, transcendentals=0)


def pairs(row_tiles):
    return [(part, number) for part in range(row_tiles) for number in range(part + 1)]


def score_tile(key_tile, value_tile, query_t, grad_t, seen=None):
    scores = dot(key_tile, query_t)
    if seen is not None:
        scores = jnp.where(seen, scores, NEG)
    top = jnp.max(scores, axis=0, keepdims=True) * FACTOR
    weights = jnp.exp2(scores * FACTOR - top)
    grad_probs = dot(value_tile, grad_t)
    total = jnp.sum(weights, axis=0, keepdims=True)
    product = jnp.sum(weights * grad_probs, axis=0, keepdims=True)
    return weights, grad_probs, (top, total, product)


def own_scores(queries, grad_out, own):
    rows, width = queries.shape
    row_tiles, heads = rows // BLK, width // HD
    places = pairs(row_tiles)
    total = heads * len(places)

    def body(q_ref, g_ref, own_ref, both_ref, qt_ref, gt_ref, weight_ref, prob_ref, stat_ref):
        both_ref[0], both_ref[1] = q_ref[...], g_ref[...]
        key_at = lax.broadcasted_iota(jnp.int32, (BLK, BLK), 0)
        causal = key_at <= lax.broadcasted_iota(jnp.int32, (BLK, BLK), 1)
        for head in range(heads):
            columns = slice(head * HD, (head + 1) * HD)
            for part in range(row_tiles):
                query_t, grad_t = q_ref[spot(part), columns].T, g_ref[spot(part), columns].T
                qt_ref[columns, spot(part)] = query_t
                gt_ref[columns, spot(part)] = grad_t
                for number in range(part + 1):
                    place = head * len(places) + places.index((part, number))
                    weight_ref[place], prob_ref[place], found = score_tile(
                        own_ref[spot(number), :HD],
                        own_ref[spot(number), HD:],
                        query_t,
                        grad_t,
                        causal if number == part else None,
                    )
                    for row, each in enumerate(found):
                        stat_ref[row, place : place + 1] = each

    tiles = jax.ShapeDtypeStruct((total, BLK, BLK), jnp.float32)
    turned = jax.ShapeDtypeStruct((width, rows), jnp.bfloat16)
    return pl.pallas_call(
        body,
        out_shape=(
            jax.ShapeDtypeStruct((2, rows, width), jnp.bfloat16),
            turned,
            turned,
            tiles,
            tiles,
            jax.ShapeDtypeStruct((3, total, BLK), jnp.float32),
        ),
        in_specs=[VMEM] * 3,
        out_specs=(VMEM,) * 6,
        compiler_params=params(8),
        cost_estimate=cost(2 * total, 2 << 20),
        name="own_scores",
    )(queries, grad_out, own)


def block_scores(queries_t, grad_t, block):
    width, rows = queries_t.shape
    row_tiles, heads = rows // BLK, width // HD

    def body(qt_ref, gt_ref, block_ref, weight_ref, prob_ref, stat_ref):
        for head in range(heads):
            columns = slice(head * HD, (head + 1) * HD)
            for part in range(row_tiles):
                place = head * row_tiles + part
                weight_ref[place], prob_ref[place], found = score_tile(
                    block_ref[:, :HD], block_ref[:, HD:], qt_ref[columns, spot(part)], gt_ref[columns, spot(part)]
                )
                for row, each in enumerate(found):
                    stat_ref[row, place : place + 1] = each

    tiles = jax.ShapeDtypeStruct((heads * row_tiles, BLK, BLK), jnp.float32)
    return pl.pallas_call(
        body,
        out_shape=(tiles, tiles, jax.ShapeDtypeStruct((3, heads * row_tiles, BLK), jnp.float32)),
        in_specs=[VMEM] * 3,
        out_specs=(VMEM,) * 3,
        compiler_params=params(8),
        cost_estimate=cost(2 * heads * row_tiles, 2 << 20),
        name="block_scores",
    )(queries_t, grad_t, block)


def kinds():
    keep = lax.axis_index("head") % 2
    scales = [jnp.where(kind == 0, SCALE, 1.0) for kind in (keep, 1 - keep)]
    return keep, 1 - keep, scales[0], scales[1]


def partner_part(both, own_stats, scored):
    _, rows, width = both.shape
    levels, row_tiles, heads = len(scored), rows // BLK, width // HD
    places = pairs(row_tiles)
    total = heads * len(places)

    def body(both_ref, own_ref, *refs):
        scored_refs = [refs[3 * level_num : 3 * level_num + 3] for level_num in range(levels)]
        send_ref, held_ref, coef_ref, chosen_ref = refs[3 * levels :]
        ctx_index = lax.axis_index("ctx")
        live = [ctx_index >= 2**level_num for level_num in range(levels)]
        ratio_of = {}
        for head in range(heads):
            for part in range(row_tiles):
                at = head * row_tiles + part
                tops, sums, products = [], [], []
                for level_num in range(levels):
                    stat_ref = scored_refs[level_num][2]
                    tops.append(jnp.where(live[level_num], stat_ref[0, at : at + 1], NEG))
                    sums.append(stat_ref[1, at : at + 1])
                    products.append(stat_ref[2, at : at + 1])
                first = head * len(places) + places.index((part, 0))
                for place in range(first, first + part + 1):
                    tops.append(own_ref[0, place : place + 1])
                    sums.append(own_ref[1, place : place + 1])
                    products.append(own_ref[2, place : place + 1])
                row_max = tops[0]
                for top in tops[1:]:
                    row_max = jnp.maximum(row_max, top)
                ratios = [jnp.exp2(top - row_max) for top in tops]
                inverse = 1.0 / sum(each * ratio for each, ratio in zip(sums, ratios))
                delta = sum(each * ratio for each, ratio in zip(products, ratios)) * inverse
                for number in range(part + 1):
                    coef_ref[first + number : first + number + 1] = ratios[levels + number] * inverse
                coef_ref[total + at : total + at + 1] = delta
                ratio_of[at] = [ratio * inverse for ratio in ratios[:levels]], delta
        _, send, _, scale = kinds()
        for level_num in range(levels):
            weight_ref, prob_ref, _ = scored_refs[level_num]
            sent = 0.0
            for head in range(heads):
                for part in range(row_tiles):
                    at = head * row_tiles + part
                    ratios, delta = ratio_of[at]
                    probs = weight_ref[at] * ratios[level_num]
                    low = (probs * (prob_ref[at] - delta)).astype(jnp.bfloat16)
                    probs = probs.astype(jnp.bfloat16)
                    held_ref[0, head, spot(level_num), spot(part)] = low
                    held_ref[1, head, spot(level_num), spot(part)] = probs
                    chosen_ref[head, spot(level_num), spot(part)] = jnp.where(send == 0, low, probs)
                columns = slice(head * HD, (head + 1) * HD)
                sent += dot(chosen_ref[head, spot(level_num)], both_ref[send, :, columns])
            send_ref[spot(level_num)] = (sent * scale).astype(jnp.bfloat16)

    return pl.pallas_call(
        body,
        out_shape=(
            jax.ShapeDtypeStruct((levels * BLK, HD), jnp.bfloat16),
            jax.ShapeDtypeStruct((2, heads, levels * BLK, rows), jnp.bfloat16),
            jax.ShapeDtypeStruct((total + heads * row_tiles, BLK), jnp.float32),
        ),
        in_specs=[VMEM] * (2 + 3 * levels),
        out_specs=(VMEM,) * 3,
        scratch_shapes=[pltpu.VMEM((heads, levels * BLK, rows), jnp.bfloat16)],
        compiler_params=params(8),
        cost_estimate=cost(2 * heads * row_tiles * levels, 2 << 20),
        name="partner_part",
    )(both, own_stats, *[each for level in scored for each in level])


def own_part(both, own, blocks, weights, grad_probs, held, coef):
    _, rows, width = both.shape
    levels, row_tiles, heads = len(blocks), rows // BLK, width // HD
    places = pairs(row_tiles)
    total = heads * len(places)

    def body(both_ref, own_ref, weight_ref, prob_ref, held_ref, coef_ref, *refs):
        block_refs = refs[:levels]
        part_ref, keep_ref, send_ref, dq_ref, kt_ref, own_held_ref = refs[levels:]
        keep, send, keep_scale, send_scale = kinds()
        for level_num in range(levels):
            kept = 0.0
            for head in range(heads):
                columns = slice(head * HD, (head + 1) * HD)
                kept += dot(held_ref[keep, head, spot(level_num)], both_ref[keep, :, columns])
            part_ref[spot(level_num)] = kept * keep_scale
        for number in range(row_tiles):
            kt_ref[:, spot(number)] = own_ref[spot(number), :HD].T
        for level_num in range(levels):
            kt_ref[:, spot(row_tiles + level_num)] = block_refs[level_num][:, :HD].T
        for head in range(heads):
            columns = slice(head * HD, (head + 1) * HD)
            for part in range(row_tiles):
                at = total + head * row_tiles + part
                delta = coef_ref[at : at + 1]
                for number in range(part + 1):
                    place = head * len(places) + places.index((part, number))
                    probs = weight_ref[place] * coef_ref[place : place + 1]
                    low = (probs * (prob_ref[place] - delta)).astype(jnp.bfloat16)
                    own_held_ref[0, head, spot(number), spot(part)] = low
                    own_held_ref[1, head, spot(number), spot(part)] = probs.astype(jnp.bfloat16)
                dq_t = dot(kt_ref[:, rows:], held_ref[0, head, :, spot(part)])
                seen = slice(0, (part + 1) * BLK)
                dq_t += dot(kt_ref[:, seen], own_held_ref[0, head, seen, spot(part)])
                dq_ref[spot(part), columns] = (dq_t * SCALE).T.astype(jnp.bfloat16)
        for number in range(row_tiles):
            kept = sent = 0.0
            seeing = slice(number * BLK, rows)
            for head in range(heads):
                columns = slice(head * HD, (head + 1) * HD)
                kept += dot(own_held_ref[keep, head, spot(number), seeing], both_ref[keep, seeing, columns])
                sent += dot(own_held_ref[send, head, spot(number), seeing], both_ref[send, seeing, columns])
            keep_ref[spot(number)] = kept * keep_scale
            send_ref[spot(number)] = (sent * send_scale).astype(jnp.bfloat16)

    return pl.pallas_call(
        body,
        out_shape=(
            jax.ShapeDtypeStruct((levels * BLK, HD), jnp.float32),
            jax.ShapeDtypeStruct((rows, HD), jnp.float32),
            jax.ShapeDtypeStruct((rows, HD), jnp.bfloat16),
            jax.ShapeDtypeStruct((rows, width), jnp.bfloat16),
        ),
        in_specs=[VMEM] * (6 + levels),
        out_specs=(VMEM,) * 4,
        scratch_shapes=[
            pltpu.VMEM((HD, rows + levels * BLK), jnp.bfloat16),
            pltpu.VMEM((2, heads, rows, rows), jnp.bfloat16),
        ],
        compiler_params=params(14),
        cost_estimate=cost(3 * total + 2 * heads * row_tiles * levels, 2 << 20),
        name="own_part",
    )(both, own, weights, grad_probs, held, coef, *blocks)


def pair_parts(kept, received, levels):
    def body(kept_ref, received_ref, *part_refs):
        for level_num in range(levels):
            total = kept_ref[spot(level_num)] + received_ref[spot(level_num)].astype(jnp.float32)
            part_refs[level_num][...] = total.astype(jnp.bfloat16)

    return pl.pallas_call(
        body,
        out_shape=(jax.ShapeDtypeStruct((BLK, HD), jnp.bfloat16),) * levels,
        in_specs=[VMEM] * 2,
        out_specs=(VMEM,) * levels,
        compiler_params=params(6),
        name="pair_parts",
    )(kept, received)


def add_returned(block_index, kept, received, returned, ctx_count):
    levels = len(returned)

    def body(index_ref, kept_ref, received_ref, *refs):
        out_ref, total_ref = refs[levels:]
        ctx_index = lax.axis_index("ctx")
        total_ref[...] = kept_ref[...] + received_ref[...].astype(jnp.float32)
        for level_num in range(levels):
            start = block_start(index_ref, ctx_index, level_num, ctx_count)
            total_ref[pl.ds(start, BLK), :] += refs[level_num][...].astype(jnp.float32)
        out_ref[...] = total_ref[...].astype(jnp.bfloat16)

    return pl.pallas_call(
        body,
        out_shape=jax.ShapeDtypeStruct(kept.shape, jnp.bfloat16),
        in_specs=[SMEM] + [VMEM] * (levels + 2),
        out_specs=VMEM,
        scratch_shapes=[pltpu.VMEM(kept.shape, jnp.float32)],
        compiler_params=params(6),
        name="add_returned",
    )(block_index, kept, received, *returned)


def lay_queries(gathered):
    count, token_rows, width = gathered.shape

    def body(in_ref, out_ref):
        for number in range(count):
            out_ref[:, number * width : (number + 1) * width] = in_ref[number]

    return pl.pallas_call(
        body,
        out_shape=jax.ShapeDtypeStruct((token_rows, count * width), gathered.dtype),
        in_specs=[VMEM],
        out_specs=VMEM,
        compiler_params=params(6),
        name="lay_queries",
    )(gathered)


def lay_keys(gathered):
    count, token_rows, _ = gathered.shape

    def body(in_ref, key_ref, value_ref):
        for number in range(count):
            kind_ref = key_ref if number % 2 == 0 else value_ref
            group = number // 2
            kind_ref[:, group * HD : (group + 1) * HD] = in_ref[number]

    shape = jax.ShapeDtypeStruct((token_rows, count // 2 * HD), gathered.dtype)
    return pl.pallas_call(
        body,
        out_shape=(shape, shape),
        in_specs=[VMEM],
        out_specs=(VMEM,) * 2,
        compiler_params=params(6),
        name="lay_keys",
    )(gathered)


def spread(value, head_count):
    split = value.reshape(head_count, value.shape[0] // head_count, value.shape[1])
    return lax.all_to_all(split, "head", split_axis=0, concat_axis=0, tiled=True)


def on_device(queries, keys, values, grad_out, block_index):
    ctx_count = lax.axis_size("ctx")
    head_count = lax.axis_size("head")
    levels = ctx_count.bit_length() - 1
    block_index = block_index.T
    hbm = [pltpu.with_memory_space_constraint(each, pltpu.HBM) for each in (block_index, keys, values)]
    own, *sends = gather_blocks(*hbm, ctx_count, levels)
    blocks = [rotate(sends[level_num], "ctx", 2**level_num) for level_num in range(levels)]
    both, queries_t, grad_t, weights, grad_probs, stats = own_scores(queries, grad_out, own)
    scored = [block_scores(queries_t, grad_t, block) for block in blocks]
    sent, held, coef = partner_part(both, stats, scored)
    received = swap(sent, "head")
    part_kept, own_kept, own_sent, dq_local = own_part(both, own, blocks, weights, grad_probs, held, coef)
    own_received = swap(own_sent, "head")
    dq_gathered = spread(dq_local, head_count)
    parts = pair_parts(part_kept, received, levels)
    returned = []
    for level_num in range(levels):
        returned.append(rotate(parts[level_num], "ctx", -(2**level_num)))
    total = add_returned(block_index, own_kept, own_received, returned, ctx_count)
    gathered = spread(total, head_count)
    grad_queries = lay_queries(dq_gathered)
    grad_keys, grad_values = lay_keys(gathered)
    return (grad_queries, grad_keys, grad_values)


def solution(mesh):
    placed = (P("ctx", "head"), P("ctx", None), P("ctx", None), P("ctx", "head"), P())
    return jax.shard_map(
        on_device,
        mesh=mesh,
        in_specs=placed,
        out_specs=(P(("ctx", "head"), None), P(("ctx", "head"), None), P(("ctx", "head"), None)),
        check_vma=False,
    )
```

profile of v0, /device:TPU:22, one launch (start us, length us, event | category | flops | bytes accessed | tf_op | source)
XLA Modules:
  0.0 78.6 jit_solution(5472011782453076107)
XLA Ops:
  0.6 0.0 copy-start.1
  0.6 0.0 copy-start.2
  0.7 1.2 %gather_blocks.1 = (bf16[1024,256]{1,0:T(8,128)(2,1)S(1)}, bf16[256,256]{1,0:T(8,128)(2,1)S(1)}, bf16[256,256]{1,0:T(8,128)(2,1)S(1)}, bf16[256,256]{1,0:T(8,128)(2,1)S(1)}, bf16[256,256]{1,0:T(8,128)(2,1)S(1)}) custom-call(s32[4,16]{1,0:T(4,128)} %bitcast.4, bf16[1024,1024]{1,0:T(8,128)(2,1)} %key_ref.1, bf16[1024,1024]{1,0:T(8,128)(2,1)} %value_ref.1), custom_call_target="tpu_custom_call" | custom-call | tf_op jit(solution)/shard_map/gather_blocks/pallas_call | solution.py:53
  1.9 0.4 collective-permute-start.3
  2.3 4.0 %collective-permute-start.2 = (bf16[256,256]{1,0:T(8,128)(2,1)S(1)}, bf16[256,256]{1,0:T(8,128)(2,1)S(1)}, u32[]{:S(2)}, u32[]{:S(2)}) collective-permute-start(bf16[256,256]{1,0:T(8,128)(2,1)S(1)} %get-tuple-element.54), channel_id=1, source_target_pairs={{0,64},{16,80},{32,96},{48,112},{64,128},{80,144},{96,160},{112,17... | collective-permute-start | bytes 393224 | tf_op jit(solution)/shard_map/ppermute | solution.py:21
  6.3 2.1 %collective-permute-start.1 = (bf16[256,256]{1,0:T(8,128)(2,1)S(1)}, bf16[256,256]{1,0:T(8,128)(2,1)S(1)}, u32[]{:S(2)}, u32[]{:S(2)}) collective-permute-start(bf16[256,256]{1,0:T(8,128)(2,1)S(1)} %get-tuple-element.50), channel_id=1, source_target_pairs={{0,32},{16,48},{32,64},{48,80},{64,96},{80,112},{96,128},{112,144}... | collective-permute-start | bytes 393224 | tf_op jit(solution)/shard_map/ppermute | solution.py:21
  8.4 0.0 collective-permute-start
  8.4 0.0 copy-done.1
  8.4 0.0 copy-done.2
  8.4 2.2 %own_scores.1 = (bf16[2,1024,256]{2,1,0:T(8,128)(2,1)S(1)}, bf16[256,1024]{1,0:T(8,128)(2,1)S(1)}, bf16[256,1024]{1,0:T(8,128)(2,1)S(1)}, f32[20,256,256]{2,1,0:...) custom-call(bf16[1024,256]{1,0:T(8,128)(2,1)S(1)} %copy-done.1, bf16[1024,256]{1,0:T(8,128)(2,1)S(1)} %copy-done.2, ...), custom_call_target="tpu_custom_call" | custom-call | flops 671088640 | bytes 2097152 | tf_op jit(solution)/shard_map/own_scores/pallas_call | solution.py:127
  10.6 0.0 collective-permute-done.3.block_ref.refs_3_
  10.6 1.0 %block_scores.7 = (f32[8,256,256]{2,1,0:T(8,128)S(1)}, f32[8,256,256]{2,1,0:T(8,128)S(1)}, f32[3,8,256]{2,1,0:T(8,128)S(1)}) custom-call(bf16[256,1024]{1,0:T(8,128)(2,1)S(1)} %get-tuple-element.44.qt_ref, bf16[256,1024]{1,0:T(8,128)(2,1)S(1)} %get-tuple-element.45.gt_ref, bf16[256,256]{1,0:T(8,128)(2,1)S(1)} %collective-permute-done.3.block_ref.refs_3_), custom_call_target="tpu_custom_call" | custom-call | flops 268435456 | bytes 2097152 | tf_op jit(solution)/shard_map/block_scores/pallas_call | solution.py:161
  11.6 0.0 collective-permute-done.2.block_ref.refs_2_
  11.6 1.0 %block_scores.6 = (f32[8,256,256]{2,1,0:T(8,128)S(1)}, f32[8,256,256]{2,1,0:T(8,128)S(1)}, f32[3,8,256]{2,1,0:T(8,128)S(1)}) custom-call(bf16[256,1024]{1,0:T(8,128)(2,1)S(1)} %get-tuple-element.44.qt_ref, bf16[256,1024]{1,0:T(8,128)(2,1)S(1)} %get-tuple-element.45.gt_ref, bf16[256,256]{1,0:T(8,128)(2,1)S(1)} %collective-permute-done.2.block_ref.refs_2_), custom_call_target="tpu_custom_call" | custom-call | flops 268435456 | bytes 2097152 | tf_op jit(solution)/shard_map/block_scores/pallas_call | solution.py:161
  12.6 0.0 collective-permute-done.1.block_ref.refs_1_
  12.6 1.0 %block_scores.5 = (f32[8,256,256]{2,1,0:T(8,128)S(1)}, f32[8,256,256]{2,1,0:T(8,128)S(1)}, f32[3,8,256]{2,1,0:T(8,128)S(1)}) custom-call(bf16[256,1024]{1,0:T(8,128)(2,1)S(1)} %get-tuple-element.44.qt_ref, bf16[256,1024]{1,0:T(8,128)(2,1)S(1)} %get-tuple-element.45.gt_ref, bf16[256,256]{1,0:T(8,128)(2,1)S(1)} %collective-permute-done.1.block_ref.refs_1_), custom_call_target="tpu_custom_call" | custom-call | flops 268435456 | bytes 2097152 | tf_op jit(solution)/shard_map/block_scores/pallas_call | solution.py:161
  13.6 0.0 collective-permute-done.block_ref.refs_0_
  13.6 0.9 %block_scores.4 = (f32[8,256,256]{2,1,0:T(8,128)S(1)}, f32[8,256,256]{2,1,0:T(8,128)S(1)}, f32[3,8,256]{2,1,0:T(8,128)S(1)}) custom-call(bf16[256,1024]{1,0:T(8,128)(2,1)S(1)} %get-tuple-element.44.qt_ref, bf16[256,1024]{1,0:T(8,128)(2,1)S(1)} %get-tuple-element.45.gt_ref, bf16[256,256]{1,0:T(8,128)(2,1)S(1)} %collective-permute-done.block_ref.refs_0_), custom_call_target="tpu_custom_call" | custom-call | flops 268435456 | bytes 2097152 | tf_op jit(solution)/shard_map/block_scores/pallas_call | solution.py:161
  14.5 2.5 %partner_part.1 = (bf16[1024,128]{1,0:T(8,128)(2,1)S(1)}, bf16[2,2,1024,1024]{3,2,1,0:T(8,128)(2,1)S(1)}, f32[28,256]{1,0:T(8,128)S(1)}) custom-call(bf16[2,1024,256]{2,1,0:T(8,128)(2,1)S(1)} %get-tuple-element.40.both_ref, f32[3,20,256]{2,1,0:T(8,128)S(1)} %get-tuple-element.43.own_ref, f32[8,256,256]{2,1,0:T(8,128)S(1)} %get-tuple-element.47.refs_0_, ...), custom_call_target="tpu_custom_call" | custom-call | flops 1073741824 | bytes 2097152 | tf_op jit(solution)/shard_map/partner_part/pallas_call | solution.py:232
  17.0 2.2 %collective-permute-start.5 = (bf16[1024,128]{1,0:T(8,128)(2,1)S(1)}, bf16[1024,128]{1,0:T(8,128)(2,1)S(1)}, u32[]{:S(2)}, u32[]{:S(2)}) collective-permute-start(bf16[1024,128]{1,0:T(8,128)(2,1)S(1)} %get-tuple-element.68), channel_id=1, source_target_pairs={{0,1},{1,0},{2,3},{3,2},{4,5},{5,4},{6,7},{7,6},{8,9},{9,8},{10,11... | collective-permute-start | bytes 786440 | tf_op jit(solution)/shard_map/ppermute | solution.py:25
  19.2 0.0 copy-start
  19.2 5.0 %own_part.1 = (f32[1024,128]{1,0:T(8,128)S(1)}, f32[1024,128]{1,0:T(8,128)S(1)}, bf16[1024,128]{1,0:T(8,128)(2,1)S(1)}, bf16[1024,256]{1,0:T(8,128)(2,1)}) custom-call(bf16[2,1024,256]{2,1,0:T(8,128)(2,1)S(1)} %get-tuple-element.40.both_ref, bf16[1024,256]{1,0:T(8,128)(2,1)S(1)} %get-tuple-element.39.own_ref, ...), custom_call_target="tpu_custom_call" | custom-call | flops 2080374784 | bytes 2097152 | tf_op jit(solution)/shard_map/own_part/pallas_call | solution.py:293
  24.1 0.1 collective-permute-start.4
  24.3 2.1 %collective-permute-done.5.received_ref = bf16[1024,128]{1,0:T(8,128)(2,1)S(1)} collective-permute-done((bf16[1024,128]{1,0:T(8,128)(2,1)S(1)}, bf16[1024,128]{1,0:T(8,128)(2,1)S(1)}, u32[]{:S(2)}, u32[]{:S(2)}) %collective-permute-start.5) | collective-permute-done | bytes 262176 | tf_op jit(solution)/shard_map/ppermute | solution.py:25
  26.3 0.1 pair_parts.1
  26.4 0.5 collective-permute-start.6
  26.8 0.0 collective-permute-start.7
  26.8 2.9 %collective-permute-start.8 = (bf16[256,128]{1,0:T(8,128)(2,1)S(1)}, bf16[256,128]{1,0:T(8,128)(2,1)S(1)}, u32[]{:S(2)}, u32[]{:S(2)}) collective-permute-start(bf16[256,128]{1,0:T(8,128)(2,1)S(1)} %get-tuple-element.71), channel_id=1, source_target_pairs={{0,192},{16,208},{32,224},{48,240},{64,0},{80,16},{96,32},{112,48}... | collective-permute-start | bytes 196616 | tf_op jit(solution)/shard_map/ppermute | solution.py:21
  29.7 4.0 %collective-permute-start.9 = (bf16[256,128]{1,0:T(8,128)(2,1)S(1)}, bf16[256,128]{1,0:T(8,128)(2,1)S(1)}, u32[]{:S(2)}, u32[]{:S(2)}) collective-permute-start(bf16[256,128]{1,0:T(8,128)(2,1)S(1)} %get-tuple-element.72), channel_id=1, source_target_pairs={{0,128},{16,144},{32,160},{48,176},{64,192},{80,208},{96,224},{112... | collective-permute-start | bytes 196616 | tf_op jit(solution)/shard_map/ppermute | solution.py:21
  33.8 0.0 collective-permute-done.4.received_ref
  33.8 0.0 collective-permute-done.6.refs_0_
  33.8 3.0 %collective-permute-done.7.refs_1_ = bf16[256,128]{1,0:T(8,128)(2,1)S(1)} collective-permute-done((bf16[256,128]{1,0:T(8,128)(2,1)S(1)}, bf16[256,128]{1,0:T(8,128)(2,1)S(1)}, u32[]{:S(2)}, u32[]{:S(2)}) %collective-permute-start.7) | collective-permute-done | bytes 65568 | tf_op jit(solution)/shard_map/ppermute | solution.py:21
  36.8 0.0 collective-permute-done.8.refs_2_
  36.8 1.3 %collective-permute-done.9.refs_3_ = bf16[256,128]{1,0:T(8,128)(2,1)S(1)} collective-permute-done((bf16[256,128]{1,0:T(8,128)(2,1)S(1)}, bf16[256,128]{1,0:T(8,128)(2,1)S(1)}, u32[]{:S(2)}, u32[]{:S(2)}) %collective-permute-start.9) | collective-permute-done | bytes 65568 | tf_op jit(solution)/shard_map/ppermute | solution.py:21
  38.1 0.0 copy-done
  38.1 0.7 add_returned.1
  38.8 19.1 %all_to_all.10.in_ref = bf16[16,64,128]{2,1,0:T(8,128)(2,1)S(1)} all-to-all(bf16[16,64,128]{2,1,0:T(8,128)(2,1)S(1)} %bitcast.3), channel_id=1, replica_groups=mesh['ctx'=16,'head'=16] {'head'}, dimensions={0} | all-to-all | bytes 524288 | tf_op jit(solution)/shard_map/all_to_all | solution.py:391
  57.9 4.5 %all-to-all-start = ((bf16[16,64,256]{2,1,0:T(8,128)(2,1)}), bf16[16,64,256]{2,1,0:T(8,128)(2,1)S(1)}, u32[]{:S(2)}, u32[]{:S(2)}) async-start(bf16[16,64,256]{2,1,0:T(8,128)(2,1)} %bitcast.1), calls=%async_computation | async-start | bytes 1048576 | tf_op jit(solution)/shard_map/all_to_all | solution.py:391
  62.4 0.8 lay_keys.1
  63.2 14.6 %all-to-all-done.in_ref = bf16[16,64,256]{2,1,0:T(8,128)(2,1)S(1)} async-done(((bf16[16,64,256]{2,1,0:T(8,128)(2,1)}), bf16[16,64,256]{2,1,0:T(8,128)(2,1)S(1)}, u32[]{:S(2)}, u32[]{:S(2)}) %all-to-all-start) | async-done | bytes 524320 | tf_op jit(solution)/shard_map/all_to_all | solution.py:391
  77.8 0.8 %lay_queries.1 = bf16[64,4096]{1,0:T(8,128)(2,1)} custom-call(bf16[16,64,256]{2,1,0:T(8,128)(2,1)S(1)} %all-to-all-done.in_ref), custom_call_target="tpu_custom_call" | custom-call | tf_op jit(solution)/shard_map/lay_queries/pallas_call | solution.py:359
Async XLA Ops:
  0.6 7.8 %copy-start.1 = (bf16[1024,256]{1,0:T(8,128)(2,1)S(1)}, bf16[1024,256]{1,0:T(8,128)(2,1)}, u32[]{:S(2)}) copy-start(bf16[1024,256]{1,0:T(8,128)(2,1)} %q_ref.1) | copy-start | bytes 1572868
  0.6 7.8 %copy-start.2 = (bf16[1024,256]{1,0:T(8,128)(2,1)S(1)}, bf16[1024,256]{1,0:T(8,128)(2,1)}, u32[]{:S(2)}) copy-start(bf16[1024,256]{1,0:T(8,128)(2,1)} %g_ref.1) | copy-start | bytes 1572868
  1.9 8.8 %collective-permute-start.3 = (bf16[256,256]{1,0:T(8,128)(2,1)S(1)}, bf16[256,256]{1,0:T(8,128)(2,1)S(1)}, u32[]{:S(2)}, u32[]{:S(2)}) collective-permute-start(bf16[256,256]{1,0:T(8,128)(2,1)S(1)} %get-tuple-element.58), channel_id=1, source_target_pairs={{0,128},{16,144},{32,160},{48,176},{64,192},{80,208},{96,224},{112... | collective-permute-start | bytes 393224 | tf_op jit(solution)/shard_map/ppermute | solution.py:21
  2.3 9.3 %collective-permute-start.2 = (bf16[256,256]{1,0:T(8,128)(2,1)S(1)}, bf16[256,256]{1,0:T(8,128)(2,1)S(1)}, u32[]{:S(2)}, u32[]{:S(2)}) collective-permute-start(bf16[256,256]{1,0:T(8,128)(2,1)S(1)} %get-tuple-element.54), channel_id=1, source_target_pairs={{0,64},{16,80},{32,96},{48,112},{64,128},{80,144},{96,160},{112,17... | collective-permute-start | bytes 393224 | tf_op jit(solution)/shard_map/ppermute | solution.py:21
  6.3 6.3 %collective-permute-start.1 = (bf16[256,256]{1,0:T(8,128)(2,1)S(1)}, bf16[256,256]{1,0:T(8,128)(2,1)S(1)}, u32[]{:S(2)}, u32[]{:S(2)}) collective-permute-start(bf16[256,256]{1,0:T(8,128)(2,1)S(1)} %get-tuple-element.50), channel_id=1, source_target_pairs={{0,32},{16,48},{32,64},{48,80},{64,96},{80,112},{96,128},{112,144}... | collective-permute-start | bytes 393224 | tf_op jit(solution)/shard_map/ppermute | solution.py:21
  8.4 5.2 %collective-permute-start = (bf16[256,256]{1,0:T(8,128)(2,1)S(1)}, bf16[256,256]{1,0:T(8,128)(2,1)S(1)}, u32[]{:S(2)}, u32[]{:S(2)}) collective-permute-start(bf16[256,256]{1,0:T(8,128)(2,1)S(1)} %get-tuple-element.46), channel_id=1, source_target_pairs={{0,16},{16,32},{32,48},{48,64},{64,80},{80,96},{96,112},{112,128},... | collective-permute-start | bytes 393224 | tf_op jit(solution)/shard_map/ppermute | solution.py:21
  17.0 9.4 %collective-permute-start.5 = (bf16[1024,128]{1,0:T(8,128)(2,1)S(1)}, bf16[1024,128]{1,0:T(8,128)(2,1)S(1)}, u32[]{:S(2)}, u32[]{:S(2)}) collective-permute-start(bf16[1024,128]{1,0:T(8,128)(2,1)S(1)} %get-tuple-element.68), channel_id=1, source_target_pairs={{0,1},{1,0},{2,3},{3,2},{4,5},{5,4},{6,7},{7,6},{8,9},{9,8},{10,11... | collective-permute-start | bytes 786440 | tf_op jit(solution)/shard_map/ppermute | solution.py:25
  19.2 18.9 %copy-start = (s32[16,4]{0,1:T(4,128)S(1)}, s32[16,4]{0,1:T(4,128)}, u32[]{:S(2)}) copy-start(s32[16,4]{0,1:T(4,128)} %param.9) | copy-start | bytes 772
  24.1 9.6 %collective-permute-start.4 = (bf16[1024,128]{1,0:T(8,128)(2,1)S(1)}, bf16[1024,128]{1,0:T(8,128)(2,1)S(1)}, u32[]{:S(2)}, u32[]{:S(2)}) collective-permute-start(bf16[1024,128]{1,0:T(8,128)(2,1)S(1)} %get-tuple-element.66), channel_id=1, source_target_pairs={{0,1},{1,0},{2,3},{3,2},{4,5},{5,4},{6,7},{7,6},{8,9},{9,8},{10,11... | collective-permute-start | bytes 786440 | tf_op jit(solution)/shard_map/ppermute | solution.py:25
  26.4 7.4 %collective-permute-start.6 = (bf16[256,128]{1,0:T(8,128)(2,1)S(1)}, bf16[256,128]{1,0:T(8,128)(2,1)S(1)}, u32[]{:S(2)}, u32[]{:S(2)}) collective-permute-start(bf16[256,128]{1,0:T(8,128)(2,1)S(1)} %get-tuple-element.69), channel_id=1, source_target_pairs={{0,240},{16,0},{32,16},{48,32},{64,48},{80,64},{96,80},{112,96},{1... | collective-permute-start | bytes 196616 | tf_op jit(solution)/shard_map/ppermute | solution.py:21
  26.8 10.0 %collective-permute-start.7 = (bf16[256,128]{1,0:T(8,128)(2,1)S(1)}, bf16[256,128]{1,0:T(8,128)(2,1)S(1)}, u32[]{:S(2)}, u32[]{:S(2)}) collective-permute-start(bf16[256,128]{1,0:T(8,128)(2,1)S(1)} %get-tuple-element.70), channel_id=1, source_target_pairs={{0,224},{16,240},{32,0},{48,16},{64,32},{80,48},{96,64},{112,80},{... | collective-permute-start | bytes 196616 | tf_op jit(solution)/shard_map/ppermute | solution.py:21
  26.8 10.0 %collective-permute-start.8 = (bf16[256,128]{1,0:T(8,128)(2,1)S(1)}, bf16[256,128]{1,0:T(8,128)(2,1)S(1)}, u32[]{:S(2)}, u32[]{:S(2)}) collective-permute-start(bf16[256,128]{1,0:T(8,128)(2,1)S(1)} %get-tuple-element.71), channel_id=1, source_target_pairs={{0,192},{16,208},{32,224},{48,240},{64,0},{80,16},{96,32},{112,48}... | collective-permute-start | bytes 196616 | tf_op jit(solution)/shard_map/ppermute | solution.py:21
  29.7 8.4 %collective-permute-start.9 = (bf16[256,128]{1,0:T(8,128)(2,1)S(1)}, bf16[256,128]{1,0:T(8,128)(2,1)S(1)}, u32[]{:S(2)}, u32[]{:S(2)}) collective-permute-start(bf16[256,128]{1,0:T(8,128)(2,1)S(1)} %get-tuple-element.72), channel_id=1, source_target_pairs={{0,128},{16,144},{32,160},{48,176},{64,192},{80,208},{96,224},{112... | collective-permute-start | bytes 196616 | tf_op jit(solution)/shard_map/ppermute | solution.py:21
  57.9 19.9 %all-to-all-start = ((bf16[16,64,256]{2,1,0:T(8,128)(2,1)}), bf16[16,64,256]{2,1,0:T(8,128)(2,1)S(1)}, u32[]{:S(2)}, u32[]{:S(2)}) async-start(bf16[16,64,256]{2,1,0:T(8,128)(2,1)} %bitcast.1), calls=%async_computation | async-start | bytes 1048576 | tf_op jit(solution)/shard_map/all_to_all | solution.py:391
where the time goes:
time: 78.8 us; the launch traced here: 78.6 us
  waiting for transfers between devices  21 us (27%)
  starting transfers between devices  20.7 us (26%)
  blocking collectives  19.1 us (24%)
  Pallas kernels  17 us (22%)
    all_to_all x1, blocking collectives, spread(): lax.all_to_all(split, 'head', split_axis=0, concat_axis=0, tiled=True)  19.1 us
    all_to_all x1, waiting for transfers between devices, spread(): lax.all_to_all(split, 'head', split_axis=0, concat_axis=0, tiled=True)  14.6 us
    ppermute x8, starting transfers between devices, rotate(): lax.ppermute(value, axis, [(source, (source + steps) % count) for source...  13.9 us
    pallas_call x1, Pallas kernels, own_part(): pl.pallas_call(body, out_shape=(jax.ShapeDtypeStruct((levels * BLK, HD),...  4.99 us
    all_to_all x1, starting transfers between devices, spread(): lax.all_to_all(split, 'head', split_axis=0, concat_axis=0, tiled=True)  4.53 us
    ppermute x8, waiting for transfers between devices, rotate(): lax.ppermute(value, axis, [(source, (source + steps) % count) for source...  4.35 us
    pallas_call x4, Pallas kernels, block_scores(): pl.pallas_call(body, out_shape=(tiles, tiles, jax.ShapeDtypeStruct((3, he...  3.82 us
    pallas_call x1, Pallas kernels, partner_part(): pl.pallas_call(body, out_shape=(jax.ShapeDtypeStruct((levels * BLK, HD),...  2.45 us
  transfers between devices with their start and end apart: 11, of which 4 were waited for; matrix products, arithmetic and copies ran while one was open for 0% of the time, Pallas kernels for 14%

commit v1 on v0

--- a/solution.py
+++ b/solution.py
@@ -119,8 +119,13 @@
                         grad_t,
                         causal if number == part else None,
                     )
+                    at = head * row_tiles + part
                     for row, each in enumerate(found):
-                        stat_ref[row, place : place + 1] = each
+                        stat_ref[row, number, at : at + 1] = each
+                for number in range(part + 1, row_tiles):
+                    at = head * row_tiles + part
+                    for row, each in enumerate((NEG, 0.0, 0.0)):
+                        stat_ref[row, number, at : at + 1] = jnp.full((1, BLK), each, jnp.float32)
 
     tiles = jax.ShapeDtypeStruct((total, BLK, BLK), jnp.float32)
     turned = jax.ShapeDtypeStruct((width, rows), jnp.bfloat16)
@@ -132,7 +137,7 @@
             turned,
             tiles,
             tiles,
-            jax.ShapeDtypeStruct((3, total, BLK), jnp.float32),
+            jax.ShapeDtypeStruct((3, row_tiles, heads * row_tiles, BLK), jnp.float32),
         ),
         in_specs=[VMEM] * 3,
         out_specs=(VMEM,) * 6,
@@ -178,39 +183,24 @@
 def partner_part(both, own_stats, scored):
     _, rows, width = both.shape
     levels, row_tiles, heads = len(scored), rows // BLK, width // HD
-    places = pairs(row_tiles)
-    total = heads * len(places)
 
     def body(both_ref, own_ref, *refs):
         scored_refs = [refs[3 * level_num : 3 * level_num + 3] for level_num in range(levels)]
         send_ref, held_ref, coef_ref, chosen_ref = refs[3 * levels :]
         ctx_index = lax.axis_index("ctx")
         live = [ctx_index >= 2**level_num for level_num in range(levels)]
-        ratio_of = {}
-        for head in range(heads):
-            for part in range(row_tiles):
-                at = head * row_tiles + part
-                tops, sums, products = [], [], []
-                for level_num in range(levels):
-                    stat_ref = scored_refs[level_num][2]
-                    tops.append(jnp.where(live[level_num], stat_ref[0, at : at + 1], NEG))
-                    sums.append(stat_ref[1, at : at + 1])
-                    products.append(stat_ref[2, at : at + 1])
-                first = head * len(places) + places.index((part, 0))
-                for place in range(first, first + part + 1):
-                    tops.append(own_ref[0, place : place + 1])
-                    sums.append(own_ref[1, place : place + 1])
-                    products.append(own_ref[2, place : place + 1])
-                row_max = tops[0]
-                for top in tops[1:]:
-                    row_max = jnp.maximum(row_max, top)
-                ratios = [jnp.exp2(top - row_max) for top in tops]
-                inverse = 1.0 / sum(each * ratio for each, ratio in zip(sums, ratios))
-                delta = sum(each * ratio for each, ratio in zip(products, ratios)) * inverse
-                for number in range(part + 1):
-                    coef_ref[first + number : first + number + 1] = ratios[levels + number] * inverse
-                coef_ref[total + at : total + at + 1] = delta
-                ratio_of[at] = [ratio * inverse for ratio in ratios[:levels]], delta
+        stats = [[level_refs[2][row] for level_refs in scored_refs] for row in range(3)]
+        tops = [jnp.where(live[level_num], stats[0][level_num], NEG) for level_num in range(levels)]
+        tops += [own_ref[0, number] for number in range(row_tiles)]
+        row_max = tops[0]
+        for top in tops[1:]:
+            row_max = jnp.maximum(row_max, top)
+        ratios = [jnp.exp2(top - row_max) for top in tops]
+        sums, products = (stats[row] + [own_ref[row, number] for number in range(row_tiles)] for row in (1, 2))
+        inverse = 1.0 / sum(each * ratio for each, ratio in zip(sums, ratios))
+        for number, ratio in enumerate(ratios):
+            coef_ref[number] = ratio * inverse
+        coef_ref[levels + row_tiles] = sum(each * ratio for each, ratio in zip(products, ratios)) * inverse
         _, send, _, scale = kinds()
         for level_num in range(levels):
             weight_ref, prob_ref, _ = scored_refs[level_num]
@@ -218,9 +208,9 @@
             for head in range(heads):
                 for part in range(row_tiles):
                     at = head * row_tiles + part
-                    ratios, delta = ratio_of[at]
-                    probs = weight_ref[at] * ratios[level_num]
-                    low = (probs * (prob_ref[at] - delta)).astype(jnp.bfloat16)
+                    row = slice(at, at + 1)
+                    probs = weight_ref[at] * coef_ref[level_num, row]
+                    low = (probs * (prob_ref[at] - coef_ref[levels + row_tiles, row])).astype(jnp.bfloat16)
                     probs = probs.astype(jnp.bfloat16)
                     held_ref[0, head, spot(level_num), spot(part)] = low
                     held_ref[1, head, spot(level_num), spot(part)] = probs
@@ -234,7 +224,7 @@
         out_shape=(
             jax.ShapeDtypeStruct((levels * BLK, HD), jnp.bfloat16),
             jax.ShapeDtypeStruct((2, heads, levels * BLK, rows), jnp.bfloat16),
-            jax.ShapeDtypeStruct((total + heads * row_tiles, BLK), jnp.float32),
+            jax.ShapeDtypeStruct((levels + row_tiles + 1, heads * row_tiles, BLK), jnp.float32),
         ),
         in_specs=[VMEM] * (2 + 3 * levels),
         out_specs=(VMEM,) * 3,
@@ -268,11 +258,12 @@
         for head in range(heads):
             columns = slice(head * HD, (head + 1) * HD)
             for part in range(row_tiles):
-                at = total + head * row_tiles + part
-                delta = coef_ref[at : at + 1]
+                at = head * row_tiles + part
+                row = slice(at, at + 1)
+                delta = coef_ref[levels + row_tiles, row]
                 for number in range(part + 1):
                     place = head * len(places) + places.index((part, number))
-                    probs = weight_ref[place] * coef_ref[place : place + 1]
+                    probs = weight_ref[place] * coef_ref[levels + number, row]
                     low = (probs * (prob_ref[place] - delta)).astype(jnp.bfloat16)
                     own_held_ref[0, head, spot(number), spot(part)] = low
                     own_held_ref[1, head, spot(number), spot(part)] = probs.astype(jnp.bfloat16)

time: 78.8 us -> 78.4 us (level)
  the two profiles are of different devices: /device:TPU:22 before, /device:TPU:62 now
where the time goes in v1:
time: 78.4 us; the launch traced here: 78.1 us
  waiting for transfers between devices  20.5 us (26%)
  starting transfers between devices  20.4 us (26%)
  blocking collectives  19.2 us (24%)
  Pallas kernels  17.2 us (22%)
    all_to_all x1, blocking collectives, spread(): lax.all_to_all(split, 'head', split_axis=0, concat_axis=0, tiled=True)  19.2 us
    all_to_all x1, waiting for transfers between devices, spread(): lax.all_to_all(split, 'head', split_axis=0, concat_axis=0, tiled=True)  14.2 us
    ppermute x8, starting transfers between devices, rotate(): lax.ppermute(value, axis, [(source, (source + steps) % count) for source...  13.4 us
    pallas_call x1, Pallas kernels, own_part(): pl.pallas_call(body, out_shape=(jax.ShapeDtypeStruct((levels * BLK, HD),...  5.31 us
    all_to_all x1, starting transfers between devices, spread(): lax.all_to_all(split, 'head', split_axis=0, concat_axis=0, tiled=True)  4.69 us
    ppermute x8, waiting for transfers between devices, rotate(): lax.ppermute(value, axis, [(source, (source + steps) % count) for source...  4.57 us
    pallas_call x4, Pallas kernels, block_scores(): pl.pallas_call(body, out_shape=(tiles, tiles, jax.ShapeDtypeStruct((3, he...  3.73 us
    pallas_call x1, Pallas kernels, partner_part(): pl.pallas_call(body, out_shape=(jax.ShapeDtypeStruct((levels * BLK, HD),...  2.4 us
  transfers between devices with their start and end apart: 11, of which 5 were waited for; matrix products, arithmetic and copies ran while one was open for 0% of the time, Pallas kernels for 14%

profile of v1, /device:TPU:62, one launch (start us, length us, event | category | flops | bytes accessed | tf_op | source)
XLA Modules:
  0.0 78.1 jit_solution(11802104266447150399)
XLA Ops:
  0.6 0.0 copy-start.1
  0.6 0.0 copy-start.2
  0.7 1.2 %gather_blocks.1 = (bf16[1024,256]{1,0:T(8,128)(2,1)S(1)}, bf16[256,256]{1,0:T(8,128)(2,1)S(1)}, bf16[256,256]{1,0:T(8,128)(2,1)S(1)}, bf16[256,256]{1,0:T(8,128)(2,1)S(1)}, bf16[256,256]{1,0:T(8,128)(2,1)S(1)}) custom-call(s32[4,16]{1,0:T(4,128)} %bitcast.4, bf16[1024,1024]{1,0:T(8,128)(2,1)} %key_ref.1, bf16[1024,1024]{1,0:T(8,128)(2,1)} %value_ref.1), custom_call_target="tpu_custom_call" | custom-call | tf_op jit(solution)/shard_map/gather_blocks/pallas_call | solution.py:53
  1.9 1.3 %collective-permute-start.3 = (bf16[256,256]{1,0:T(8,128)(2,1)S(1)}, bf16[256,256]{1,0:T(8,128)(2,1)S(1)}, u32[]{:S(2)}, u32[]{:S(2)}) collective-permute-start(bf16[256,256]{1,0:T(8,128)(2,1)S(1)} %get-tuple-element.58), channel_id=1, source_target_pairs={{0,128},{16,144},{32,160},{48,176},{64,192},{80,208},{96,224},{112... | collective-permute-start | bytes 393224 | tf_op jit(solution)/shard_map/ppermute | solution.py:21
  3.2 3.1 %collective-permute-start.2 = (bf16[256,256]{1,0:T(8,128)(2,1)S(1)}, bf16[256,256]{1,0:T(8,128)(2,1)S(1)}, u32[]{:S(2)}, u32[]{:S(2)}) collective-permute-start(bf16[256,256]{1,0:T(8,128)(2,1)S(1)} %get-tuple-element.54), channel_id=1, source_target_pairs={{0,64},{16,80},{32,96},{48,112},{64,128},{80,144},{96,160},{112,17... | collective-permute-start | bytes 393224 | tf_op jit(solution)/shard_map/ppermute | solution.py:21
  6.3 2.1 %collective-permute-start.1 = (bf16[256,256]{1,0:T(8,128)(2,1)S(1)}, bf16[256,256]{1,0:T(8,128)(2,1)S(1)}, u32[]{:S(2)}, u32[]{:S(2)}) collective-permute-start(bf16[256,256]{1,0:T(8,128)(2,1)S(1)} %get-tuple-element.50), channel_id=1, source_target_pairs={{0,32},{16,48},{32,64},{48,80},{64,96},{80,112},{96,128},{112,144}... | collective-permute-start | bytes 393224 | tf_op jit(solution)/shard_map/ppermute | solution.py:21
  8.4 0.0 collective-permute-start
  8.4 0.0 copy-done.1
  8.4 0.0 copy-done.2
  8.4 2.2 %own_scores.1 = (bf16[2,1024,256]{2,1,0:T(8,128)(2,1)S(1)}, bf16[256,1024]{1,0:T(8,128)(2,1)S(1)}, bf16[256,1024]{1,0:T(8,128)(2,1)S(1)}, f32[20,256,256]{2,1,0:...) custom-call(bf16[1024,256]{1,0:T(8,128)(2,1)S(1)} %copy-done.1, bf16[1024,256]{1,0:T(8,128)(2,1)S(1)} %copy-done.2, ...), custom_call_target="tpu_custom_call" | custom-call | flops 671088640 | bytes 2097152 | tf_op jit(solution)/shard_map/own_scores/pallas_call | solution.py:132
  10.6 0.0 collective-permute-done.3.block_ref.refs_3_
  10.6 1.0 %block_scores.7 = (f32[8,256,256]{2,1,0:T(8,128)S(1)}, f32[8,256,256]{2,1,0:T(8,128)S(1)}, f32[3,8,256]{2,1,0:T(8,128)S(1)}) custom-call(bf16[256,1024]{1,0:T(8,128)(2,1)S(1)} %get-tuple-element.44.qt_ref, bf16[256,1024]{1,0:T(8,128)(2,1)S(1)} %get-tuple-element.45.gt_ref, bf16[256,256]{1,0:T(8,128)(2,1)S(1)} %collective-permute-done.3.block_ref.refs_3_), custom_call_target="tpu_custom_call" | custom-call | flops 268435456 | bytes 2097152 | tf_op jit(solution)/shard_map/block_scores/pallas_call | solution.py:166
  11.6 0.0 collective-permute-done.2.block_ref.refs_2_
  11.6 0.9 %block_scores.6 = (f32[8,256,256]{2,1,0:T(8,128)S(1)}, f32[8,256,256]{2,1,0:T(8,128)S(1)}, f32[3,8,256]{2,1,0:T(8,128)S(1)}) custom-call(bf16[256,1024]{1,0:T(8,128)(2,1)S(1)} %get-tuple-element.44.qt_ref, bf16[256,1024]{1,0:T(8,128)(2,1)S(1)} %get-tuple-element.45.gt_ref, bf16[256,256]{1,0:T(8,128)(2,1)S(1)} %collective-permute-done.2.block_ref.refs_2_), custom_call_target="tpu_custom_call" | custom-call | flops 268435456 | bytes 2097152 | tf_op jit(solution)/shard_map/block_scores/pallas_call | solution.py:166
  12.5 0.1 collective-permute-done.1.block_ref.refs_1_
  12.6 0.9 %block_scores.5 = (f32[8,256,256]{2,1,0:T(8,128)S(1)}, f32[8,256,256]{2,1,0:T(8,128)S(1)}, f32[3,8,256]{2,1,0:T(8,128)S(1)}) custom-call(bf16[256,1024]{1,0:T(8,128)(2,1)S(1)} %get-tuple-element.44.qt_ref, bf16[256,1024]{1,0:T(8,128)(2,1)S(1)} %get-tuple-element.45.gt_ref, bf16[256,256]{1,0:T(8,128)(2,1)S(1)} %collective-permute-done.1.block_ref.refs_1_), custom_call_target="tpu_custom_call" | custom-call | flops 268435456 | bytes 2097152 | tf_op jit(solution)/shard_map/block_scores/pallas_call | solution.py:166
  13.5 0.0 collective-permute-done.block_ref.refs_0_
  13.6 0.9 %block_scores.4 = (f32[8,256,256]{2,1,0:T(8,128)S(1)}, f32[8,256,256]{2,1,0:T(8,128)S(1)}, f32[3,8,256]{2,1,0:T(8,128)S(1)}) custom-call(bf16[256,1024]{1,0:T(8,128)(2,1)S(1)} %get-tuple-element.44.qt_ref, bf16[256,1024]{1,0:T(8,128)(2,1)S(1)} %get-tuple-element.45.gt_ref, bf16[256,256]{1,0:T(8,128)(2,1)S(1)} %collective-permute-done.block_ref.refs_0_), custom_call_target="tpu_custom_call" | custom-call | flops 268435456 | bytes 2097152 | tf_op jit(solution)/shard_map/block_scores/pallas_call | solution.py:166
  14.5 2.4 %partner_part.1 = (bf16[1024,128]{1,0:T(8,128)(2,1)S(1)}, bf16[2,2,1024,1024]{3,2,1,0:T(8,128)(2,1)S(1)}, f32[9,8,256]{2,1,0:T(8,128)S(1)}) custom-call(bf16[2,1024,256]{2,1,0:T(8,128)(2,1)S(1)} %get-tuple-element.40.both_ref, f32[3,4,8,256]{3,2,1,0:T(8,128)S(1)} %get-tuple-element.43.own_ref, f32[8,256,256]{2,1,0:T(8,128)S(1)} %get-tuple-element.47.refs_0_, ...), custom_call_target="tpu_custom_call" | custom-call | flops 1073741824 | bytes 2097152 | tf_op jit(solution)/shard_map/partner_part/pallas_call | solution.py:222
  16.9 0.4 collective-permute-start.5
  17.2 0.0 copy-start
  17.3 5.3 %own_part.1 = (f32[1024,128]{1,0:T(8,128)S(1)}, f32[1024,128]{1,0:T(8,128)S(1)}, bf16[1024,128]{1,0:T(8,128)(2,1)S(1)}, bf16[1024,256]{1,0:T(8,128)(2,1)}) custom-call(bf16[2,1024,256]{2,1,0:T(8,128)(2,1)S(1)} %get-tuple-element.40.both_ref, bf16[1024,256]{1,0:T(8,128)(2,1)S(1)} %get-tuple-element.39.own_ref, ...), custom_call_target="tpu_custom_call" | custom-call | flops 2080374784 | bytes 2097152 | tf_op jit(solution)/shard_map/own_part/pallas_call | solution.py:284
  22.6 1.9 %collective-permute-start.4 = (bf16[1024,128]{1,0:T(8,128)(2,1)S(1)}, bf16[1024,128]{1,0:T(8,128)(2,1)S(1)}, u32[]{:S(2)}, u32[]{:S(2)}) collective-permute-start(bf16[1024,128]{1,0:T(8,128)(2,1)S(1)} %get-tuple-element.66), channel_id=1, source_target_pairs={{0,1},{1,0},{2,3},{3,2},{4,5},{5,4},{6,7},{7,6},{8,9},{9,8},{10,11... | collective-permute-start | bytes 786440 | tf_op jit(solution)/shard_map/ppermute | solution.py:25
  24.5 1.8 %collective-permute-done.5.received_ref = bf16[1024,128]{1,0:T(8,128)(2,1)S(1)} collective-permute-done((bf16[1024,128]{1,0:T(8,128)(2,1)S(1)}, bf16[1024,128]{1,0:T(8,128)(2,1)S(1)}, u32[]{:S(2)}, u32[]{:S(2)}) %collective-permute-start.5) | collective-permute-done | bytes 262176 | tf_op jit(solution)/shard_map/ppermute | solution.py:25
  26.3 0.1 pair_parts.1
  26.3 1.0 %collective-permute-start.6 = (bf16[256,128]{1,0:T(8,128)(2,1)S(1)}, bf16[256,128]{1,0:T(8,128)(2,1)S(1)}, u32[]{:S(2)}, u32[]{:S(2)}) collective-permute-start(bf16[256,128]{1,0:T(8,128)(2,1)S(1)} %get-tuple-element.69), channel_id=1, source_target_pairs={{0,240},{16,0},{32,16},{48,32},{64,48},{80,64},{96,80},{112,96},{1... | collective-permute-start | bytes 196616 | tf_op jit(solution)/shard_map/ppermute | solution.py:21
  27.3 0.4 collective-permute-start.7
  27.7 3.2 %collective-permute-start.8 = (bf16[256,128]{1,0:T(8,128)(2,1)S(1)}, bf16[256,128]{1,0:T(8,128)(2,1)S(1)}, u32[]{:S(2)}, u32[]{:S(2)}) collective-permute-start(bf16[256,128]{1,0:T(8,128)(2,1)S(1)} %get-tuple-element.71), channel_id=1, source_target_pairs={{0,192},{16,208},{32,224},{48,240},{64,0},{80,16},{96,32},{112,48}... | collective-permute-start | bytes 196616 | tf_op jit(solution)/shard_map/ppermute | solution.py:21
  30.9 2.3 %collective-permute-start.9 = (bf16[256,128]{1,0:T(8,128)(2,1)S(1)}, bf16[256,128]{1,0:T(8,128)(2,1)S(1)}, u32[]{:S(2)}, u32[]{:S(2)}) collective-permute-start(bf16[256,128]{1,0:T(8,128)(2,1)S(1)} %get-tuple-element.72), channel_id=1, source_target_pairs={{0,128},{16,144},{32,160},{48,176},{64,192},{80,208},{96,224},{112... | collective-permute-start | bytes 196616 | tf_op jit(solution)/shard_map/ppermute | solution.py:21
  33.2 0.0 collective-permute-done.4.received_ref
  33.2 0.0 collective-permute-done.6.refs_0_
  33.2 3.4 %collective-permute-done.7.refs_1_ = bf16[256,128]{1,0:T(8,128)(2,1)S(1)} collective-permute-done((bf16[256,128]{1,0:T(8,128)(2,1)S(1)}, bf16[256,128]{1,0:T(8,128)(2,1)S(1)}, u32[]{:S(2)}, u32[]{:S(2)}) %collective-permute-start.7) | collective-permute-done | bytes 65568 | tf_op jit(solution)/shard_map/ppermute | solution.py:21
  36.6 0.0 collective-permute-done.8.refs_2_
  36.6 1.1 %collective-permute-done.9.refs_3_ = bf16[256,128]{1,0:T(8,128)(2,1)S(1)} collective-permute-done((bf16[256,128]{1,0:T(8,128)(2,1)S(1)}, bf16[256,128]{1,0:T(8,128)(2,1)S(1)}, u32[]{:S(2)}, u32[]{:S(2)}) %collective-permute-start.9) | collective-permute-done | bytes 65568 | tf_op jit(solution)/shard_map/ppermute | solution.py:21
  37.7 0.0 copy-done
  37.7 0.7 add_returned.1
  38.4 19.2 %all_to_all.10.in_ref = bf16[16,64,128]{2,1,0:T(8,128)(2,1)S(1)} all-to-all(bf16[16,64,128]{2,1,0:T(8,128)(2,1)S(1)} %bitcast.3), channel_id=1, replica_groups=mesh['ctx'=16,'head'=16] {'head'}, dimensions={0} | all-to-all | bytes 524288 | tf_op jit(solution)/shard_map/all_to_all | solution.py:382
  57.6 4.7 %all-to-all-start = ((bf16[16,64,256]{2,1,0:T(8,128)(2,1)}), bf16[16,64,256]{2,1,0:T(8,128)(2,1)S(1)}, u32[]{:S(2)}, u32[]{:S(2)}) async-start(bf16[16,64,256]{2,1,0:T(8,128)(2,1)} %bitcast.1), calls=%async_computation | async-start | bytes 1048576 | tf_op jit(solution)/shard_map/all_to_all | solution.py:382
  62.3 0.8 lay_keys.1
  63.1 14.2 %all-to-all-done.in_ref = bf16[16,64,256]{2,1,0:T(8,128)(2,1)S(1)} async-done(((bf16[16,64,256]{2,1,0:T(8,128)(2,1)}), bf16[16,64,256]{2,1,0:T(8,128)(2,1)S(1)}, u32[]{:S(2)}, u32[]{:S(2)}) %all-to-all-start) | async-done | bytes 524320 | tf_op jit(solution)/shard_map/all_to_all | solution.py:382
  77.3 0.8 %lay_queries.1 = bf16[64,4096]{1,0:T(8,128)(2,1)} custom-call(bf16[16,64,256]{2,1,0:T(8,128)(2,1)S(1)} %all-to-all-done.in_ref), custom_call_target="tpu_custom_call" | custom-call | tf_op jit(solution)/shard_map/lay_queries/pallas_call | solution.py:350
Async XLA Ops:
  0.6 7.8 %copy-start.1 = (bf16[1024,256]{1,0:T(8,128)(2,1)S(1)}, bf16[1024,256]{1,0:T(8,128)(2,1)}, u32[]{:S(2)}) copy-start(bf16[1024,256]{1,0:T(8,128)(2,1)} %q_ref.1) | copy-start | bytes 1572868
  0.6 7.8 %copy-start.2 = (bf16[1024,256]{1,0:T(8,128)(2,1)S(1)}, bf16[1024,256]{1,0:T(8,128)(2,1)}, u32[]{:S(2)}) copy-start(bf16[1024,256]{1,0:T(8,128)(2,1)} %g_ref.1) | copy-start | bytes 1572868
  1.9 8.8 %collective-permute-start.3 = (bf16[256,256]{1,0:T(8,128)(2,1)S(1)}, bf16[256,256]{1,0:T(8,128)(2,1)S(1)}, u32[]{:S(2)}, u32[]{:S(2)}) collective-permute-start(bf16[256,256]{1,0:T(8,128)(2,1)S(1)} %get-tuple-element.58), channel_id=1, source_target_pairs={{0,128},{16,144},{32,160},{48,176},{64,192},{80,208},{96,224},{112... | collective-permute-start | bytes 393224 | tf_op jit(solution)/shard_map/ppermute | solution.py:21
  3.2 8.4 %collective-permute-start.2 = (bf16[256,256]{1,0:T(8,128)(2,1)S(1)}, bf16[256,256]{1,0:T(8,128)(2,1)S(1)}, u32[]{:S(2)}, u32[]{:S(2)}) collective-permute-start(bf16[256,256]{1,0:T(8,128)(2,1)S(1)} %get-tuple-element.54), channel_id=1, source_target_pairs={{0,64},{16,80},{32,96},{48,112},{64,128},{80,144},{96,160},{112,17... | collective-permute-start | bytes 393224 | tf_op jit(solution)/shard_map/ppermute | solution.py:21
  6.3 6.3 %collective-permute-start.1 = (bf16[256,256]{1,0:T(8,128)(2,1)S(1)}, bf16[256,256]{1,0:T(8,128)(2,1)S(1)}, u32[]{:S(2)}, u32[]{:S(2)}) collective-permute-start(bf16[256,256]{1,0:T(8,128)(2,1)S(1)} %get-tuple-element.50), channel_id=1, source_target_pairs={{0,32},{16,48},{32,64},{48,80},{64,96},{80,112},{96,128},{112,144}... | collective-permute-start | bytes 393224 | tf_op jit(solution)/shard_map/ppermute | solution.py:21
  8.4 5.1 %collective-permute-start = (bf16[256,256]{1,0:T(8,128)(2,1)S(1)}, bf16[256,256]{1,0:T(8,128)(2,1)S(1)}, u32[]{:S(2)}, u32[]{:S(2)}) collective-permute-start(bf16[256,256]{1,0:T(8,128)(2,1)S(1)} %get-tuple-element.46), channel_id=1, source_target_pairs={{0,16},{16,32},{32,48},{48,64},{64,80},{80,96},{96,112},{112,128},... | collective-permute-start | bytes 393224 | tf_op jit(solution)/shard_map/ppermute | solution.py:21
  16.9 9.4 %collective-permute-start.5 = (bf16[1024,128]{1,0:T(8,128)(2,1)S(1)}, bf16[1024,128]{1,0:T(8,128)(2,1)S(1)}, u32[]{:S(2)}, u32[]{:S(2)}) collective-permute-start(bf16[1024,128]{1,0:T(8,128)(2,1)S(1)} %get-tuple-element.68), channel_id=1, source_target_pairs={{0,1},{1,0},{2,3},{3,2},{4,5},{5,4},{6,7},{7,6},{8,9},{9,8},{10,11... | collective-permute-start | bytes 786440 | tf_op jit(solution)/shard_map/ppermute | solution.py:25
  17.2 20.5 %copy-start = (s32[16,4]{0,1:T(4,128)S(1)}, s32[16,4]{0,1:T(4,128)}, u32[]{:S(2)}) copy-start(s32[16,4]{0,1:T(4,128)} %param.9) | copy-start | bytes 772
  22.6 10.7 %collective-permute-start.4 = (bf16[1024,128]{1,0:T(8,128)(2,1)S(1)}, bf16[1024,128]{1,0:T(8,128)(2,1)S(1)}, u32[]{:S(2)}, u32[]{:S(2)}) collective-permute-start(bf16[1024,128]{1,0:T(8,128)(2,1)S(1)} %get-tuple-element.66), channel_id=1, source_target_pairs={{0,1},{1,0},{2,3},{3,2},{4,5},{5,4},{6,7},{7,6},{8,9},{9,8},{10,11... | collective-permute-start | bytes 786440 | tf_op jit(solution)/shard_map/ppermute | solution.py:25
  26.3 6.9 %collective-permute-start.6 = (bf16[256,128]{1,0:T(8,128)(2,1)S(1)}, bf16[256,128]{1,0:T(8,128)(2,1)S(1)}, u32[]{:S(2)}, u32[]{:S(2)}) collective-permute-start(bf16[256,128]{1,0:T(8,128)(2,1)S(1)} %get-tuple-element.69), channel_id=1, source_target_pairs={{0,240},{16,0},{32,16},{48,32},{64,48},{80,64},{96,80},{112,96},{1... | collective-permute-start | bytes 196616 | tf_op jit(solution)/shard_map/ppermute | solution.py:21
  27.3 9.3 %collective-permute-start.7 = (bf16[256,128]{1,0:T(8,128)(2,1)S(1)}, bf16[256,128]{1,0:T(8,128)(2,1)S(1)}, u32[]{:S(2)}, u32[]{:S(2)}) collective-permute-start(bf16[256,128]{1,0:T(8,128)(2,1)S(1)} %get-tuple-element.70), channel_id=1, source_target_pairs={{0,224},{16,240},{32,0},{48,16},{64,32},{80,48},{96,64},{112,80},{... | collective-permute-start | bytes 196616 | tf_op jit(solution)/shard_map/ppermute | solution.py:21
  27.7 8.9 %collective-permute-start.8 = (bf16[256,128]{1,0:T(8,128)(2,1)S(1)}, bf16[256,128]{1,0:T(8,128)(2,1)S(1)}, u32[]{:S(2)}, u32[]{:S(2)}) collective-permute-start(bf16[256,128]{1,0:T(8,128)(2,1)S(1)} %get-tuple-element.71), channel_id=1, source_target_pairs={{0,192},{16,208},{32,224},{48,240},{64,0},{80,16},{96,32},{112,48}... | collective-permute-start | bytes 196616 | tf_op jit(solution)/shard_map/ppermute | solution.py:21
  30.9 6.8 %collective-permute-start.9 = (bf16[256,128]{1,0:T(8,128)(2,1)S(1)}, bf16[256,128]{1,0:T(8,128)(2,1)S(1)}, u32[]{:S(2)}, u32[]{:S(2)}) collective-permute-start(bf16[256,128]{1,0:T(8,128)(2,1)S(1)} %get-tuple-element.72), channel_id=1, source_target_pairs={{0,128},{16,144},{32,160},{48,176},{64,192},{80,208},{96,224},{112... | collective-permute-start | bytes 196616 | tf_op jit(solution)/shard_map/ppermute | solution.py:21
  57.6 19.6 %all-to-all-start = ((bf16[16,64,256]{2,1,0:T(8,128)(2,1)}), bf16[16,64,256]{2,1,0:T(8,128)(2,1)S(1)}, u32[]{:S(2)}, u32[]{:S(2)}) async-start(bf16[16,64,256]{2,1,0:T(8,128)(2,1)} %bitcast.1), calls=%async_computation | async-start | bytes 1048576 | tf_op jit(solution)/shard_map/all_to_all | solution.py:382
